TPU v7x, 32 devices: a whole 2x2x4 slice. The times are simulated.
32 devices in a mesh: chan: 8 (over y, x, core), win: 4 (over z).
Axes of the slice: x: 2, y: 2, z: 4, core: 2. Of those that a mesh axis runs over, the one named last changes fastest.
Arguments:
- records: float32 [16, 1024, 256], P('win', 'chan'), may hold values from -180 to 180
- sources: int32 [32], replicated, may hold values from 0 to 255, as said below
Outputs:
- correlations: float32 [32, 256, 256], P('win', None, 'chan')
Inputs may be any that keep to these rules, and one draw needn't show every extreme that they name: `sources`: source s is one of the channels s * 8 to (s + 1) * 8 - 1; the first source is channel 0 and the last is channel 256 - 1.
All inputs are finite; a program needn't handle non-finite values.
Results may differ from a plain program's by a relative error of at most 0.00022.
Values sent between devices are 32-bit elements; how exact they have to be, the bound alone decides.
A program may use at most 64 MiB of HBM per device.

v0:
```python
import math
import jax
import jax.numpy as jnp
from jax import lax
from jax.sharding import PartitionSpec as P

HIGHEST = lax.Precision.HIGHEST
AMPLITUDE_FLOOR = 0.25
WHITE_EPSILON = 1e-06


def fourier_table(length):
    freq_count = length // 2
    freqs = jnp.arange(freq_count, dtype=jnp.int32)[:, None]
    sample_index = jnp.arange(length, dtype=jnp.int32)[None, :]
    angles = (freqs * sample_index % length).astype(jnp.float32) * (2.0 * math.pi / length)
    return jnp.concatenate([jnp.cos(angles), -jnp.sin(angles)], axis=0)


def band_table(freq_count, reach):
    rows_index = jnp.arange(freq_count, dtype=jnp.int32)[:, None]
    cols_index = jnp.arange(freq_count, dtype=jnp.int32)[None, :]
    return (jnp.abs(rows_index - cols_index) <= reach).astype(jnp.float32)


def inverse_table(length, lag_count, first_bin, bin_count, factor):
    freqs = first_bin + jnp.arange(bin_count, dtype=jnp.int32)
    lag_index = jnp.arange(lag_count, dtype=jnp.int32) - lag_count // 2
    angles = (lag_index[:, None] * freqs[None, :] % length).astype(jnp.float32) * (
        2.0 * math.pi / length
    )
    weights = jnp.where(freqs == 0, 1.0, 2.0).astype(jnp.float32)[None, :] * factor
    return jnp.concatenate([weights * jnp.cos(angles), -weights * jnp.sin(angles)], axis=1)


def running_level(padded, time_count, window_span):
    window_total = padded.shape[0]
    chans = padded.shape[2]
    running = jnp.concatenate(
        [jnp.zeros((window_total, 1, chans), jnp.float32), jnp.cumsum(jnp.abs(padded), axis=1)],
        axis=1,
    )
    return (running[:, window_span:] - running[:, :time_count]) / window_span


def local(records, sources):
    chan_count = lax.axis_size("chan")
    local_windows, local_time, all_channels = records.shape
    length = local_time * chan_count
    freq_count = length // 2
    chan_width = all_channels // chan_count
    half_width = min(16, local_time)
    smooth_reach = length // 32
    window_span = 2 * half_width + 1
    lag_count = length // 4
    forward = fourier_table(length)
    band_matrix = band_table(freq_count, smooth_reach)
    pieces = lax.all_to_all(records, "chan", split_axis=2, concat_axis=1, tiled=True)
    padded = jnp.pad(pieces, ((0, 0), (half_width, half_width), (0, 0)))
    amplitude = running_level(padded, length, window_span)
    whiten_pieces = pieces / jnp.maximum(amplitude, AMPLITUDE_FLOOR)
    spectrum = jnp.einsum("kt,wtc->wkc", forward, whiten_pieces, precision=HIGHEST)
    real_part = spectrum[:, :freq_count]
    imag_part = spectrum[:, freq_count:]
    magnitude = jnp.sqrt(real_part * real_part + imag_part * imag_part)
    smoothed = (
        jnp.einsum("jk,wkc->wjc", band_matrix, magnitude, precision=HIGHEST)
        / (2 * smooth_reach + 1)
        + WHITE_EPSILON
    )
    whitened = jnp.stack([real_part / smoothed, imag_part / smoothed], axis=1)
    band_data = lax.all_to_all(whitened, "win", split_axis=2, concat_axis=0, tiled=True)
    total_windows = band_data.shape[0]
    band_count = band_data.shape[2]
    source_count = sources.shape[0]
    chan_index = lax.axis_index("chan")
    channel_ids = jnp.arange(chan_width, dtype=jnp.int32)
    per_device = source_count // chan_count
    owned_local = (
        lax.dynamic_slice_in_dim(sources, chan_index * per_device, per_device)
        - chan_index * chan_width
    )
    selector = (owned_local[:, None] == channel_ids[None, :]).astype(jnp.float32)
    chosen = jnp.einsum("sc,wafc->wafs", selector, band_data, precision=HIGHEST)
    spectra = lax.all_gather(chosen, "chan", axis=3, tiled=True)
    source_real = spectra[:, 0]
    source_imag = spectra[:, 1]
    white_real = band_data[:, 0]
    white_imag = band_data[:, 1]
    cross_real = jnp.einsum(
        "wfs,wfc->fsc", source_real, white_real, precision=HIGHEST
    ) + jnp.einsum("wfs,wfc->fsc", source_imag, white_imag, precision=HIGHEST)
    cross_imag = jnp.einsum(
        "wfs,wfc->fsc", source_real, white_imag, precision=HIGHEST
    ) - jnp.einsum("wfs,wfc->fsc", source_imag, white_real, precision=HIGHEST)
    stacked = jnp.stack([cross_real, cross_imag])
    factor = 1.0 / math.sqrt(total_windows * freq_count)
    band_start = lax.axis_index("win") * band_count
    band_table_part = inverse_table(length, lag_count, band_start, band_count, factor).reshape(
        lag_count, 2, band_count
    )
    return lax.psum_scatter(
        jnp.einsum("tak,aksc->stc", band_table_part, stacked, precision=HIGHEST),
        "win",
        scatter_dimension=0,
        tiled=True,
    )


def solution(mesh):
    placed = (P("win", "chan", None), P())
    return jax.shard_map(
        local, mesh=mesh, in_specs=placed, out_specs=P("win", None, "chan"), check_vma=False
    )
```

profile of v0, /device:TPU:0, one launch (start us, length us, event | category | flops | bytes accessed | tf_op | source)
XLA Modules:
  0.0 168.4 jit_solution(1420910097086612107)
XLA Ops:
  6.5 2.1 %copy.58 = f32[4,128,256]{1,0,2:T(4,128)} copy(f32[4,128,256]{2,1,0:T(8,128)} %param.2) | data formatting | bytes 1048576 | tf_op args[0]
  8.6 5.2 %all-to-all-start = ((f32[4,128,256]{1,0,2:T(4,128)}), f32[4,128,256]{1,0,2:T(4,128)S(1)}, u32[]{:S(2)}, u32[]{:S(2)}) async-start(f32[4,128,256]{1,0,2:T(4,128)} %copy.58), calls=%async_computation | async-start | bytes 1048576 | tf_op jit(solution)/shard_map/all_to_all | solution.py:58
  13.8 9.2 %sine_negate_fusion = (f32[512,1024]{1,0:T(8,128)}, f32[512,1024]{1,0:T(8,128)}) fusion(), kind=kLoop, calls=%fused_computation.15 | loop fusion | flops 7864320 | bytes 4194304 | tf_op jit(solution)/shard_map/neg | solution.py:17
  23.0 0.5 all-to-all-done
  24.0 36.3 %reduce-window.6 = f32[4,32,9,128]{3,2,1,0:T(8,128)S(1)} reduce-window(f32[4,32,9,128]{3,2,1,0:T(8,128)S(1)} %reshape.194, f32[]{:T(128)} %constant.22.clone.1), window={size=1x1x1x128 pad=0_0x0_0x0_0x127_0}, to_apply=%region_0.1 | reduce-window | flops 18726912 | bytes 1179652 | tf_op jit(solution)/shard_map/reduce-window
  60.3 0.3 slice.45
  60.6 0.4 copy.61
  61.1 0.3 broadcast_add_fusion
  61.5 6.6 %fusion.14 = f32[4,1024,32]{1,2,0:T(8,128)S(1)} fusion(f32[512,1024]{1,0:T(8,128)} %get-tuple-element.13, f32[512,1024]{1,0:T(8,128)} %get-tuple-element.14, f32[4,1056,32]{1,2,0:T(8,128)S(1)} %bitcast.87, f32[4,1152,32]{1,2,0:T(8,128)S(1)} %bitcast.86, f32[4,8,4,8,128]{4,3,2,1,0:T(8,128)S(1)} %bitcast.84), kind=kOutput, calls=%fused_computation.20 | convolution fusion | flops 1612185600 | bytes 6356992 | tf_op jit(solution)/shard_map/kt,wtc->wkc/dot_general | solution.py:62
  68.1 0.7 divide_bitcast_fusion.1
  68.9 1.1 copy.63
  70.0 2.1 %reshape.201 = f32[4,1,32768]{2,1,0:T(1,128)} reshape(f32[512,2,4,32]{3,2,1,0:T(4,128)S(1)} %bitcast.79) | data formatting | bytes 1048576
  72.0 4.9 %all-to-all-start.1 = ((f32[4,1,32768]{2,1,0:T(1,128)}), f32[4,1,32768]{2,1,0:T(1,128)S(1)}, u32[]{:S(2)}, u32[]{:S(2)}) async-start(f32[4,1,32768]{2,1,0:T(1,128)} %reshape.201), calls=%async_computation.1 | async-start | bytes 1048576 | tf_op jit(solution)/shard_map/all_to_all | solution.py:72
  77.0 1.3 cosine_multiply_fusion
  78.2 13.3 %all-to-all-done.1 = f32[4,1,32768]{2,1,0:T(1,128)S(1)} async-done(((f32[4,1,32768]{2,1,0:T(1,128)}), f32[4,1,32768]{2,1,0:T(1,128)S(1)}, u32[]{:S(2)}, u32[]{:S(2)}) %all-to-all-start.1) | async-done | bytes 524320 | tf_op jit(solution)/shard_map/all_to_all | solution.py:72
  91.5 0.5 broadcast.245
  92.0 2.1 %reduce = f32[4,32768]{1,0:T(4,128)S(1)} reduce(f32[4,1,32768]{2,1,0:T(1,128)S(1)} %all-to-all-done.1, f32[]{:T(128)} %broadcast.245), dimensions={1}, to_apply=%all_to_all.30.reduce_sub_computation | reduce | bytes 1048580 | tf_op jit(solution)/shard_map/all_to_all | solution.py:72
  94.2 1.1 reshape.202
  95.3 0.8 copy.64
  96.5 10.0 %all_gather.3 = f32[16,2,128,32]{2,0,1,3:T(8,128)S(1)} all-gather(f32[16,2,128,4]{2,0,1,3:T(8,128)S(1)} %copy.65), channel_id=1, replica_groups=mesh['chan'=8,'win'=4] {'chan'}, dimensions={3}, use_global_device_ids=true | all-gather | bytes 589824 | tf_op jit(solution)/shard_map/all_gather | solution.py:85
  106.5 0.7 fusion.60
  107.2 0.5 copy.77
  107.7 0.5 copy.67
  108.2 1.5 copy.78
  109.7 1.4 copy.69
  111.1 3.6 %fusion.21 = f32[128,32,32]{2,1,0:T(8,128)S(1)} fusion(f32[16,128,32]{2,0,1:T(8,128)S(1)} %copy.67, f32[16,1,128,32]{3,0,2,1:T(8,128)S(1)} %copy.77), kind=kOutput, calls=%fused_computation.28 | convolution fusion | flops 25165824 | bytes 1048576 | tf_op jit(solution)/shard_map/wfs,wfc->fsc/dot_general | solution.py:90
  114.7 3.6 %fusion.19 = f32[128,32,32]{2,1,0:T(8,128)S(1)} fusion(f32[16,128,32]{2,0,1:T(8,128)S(1)} %copy-done, f32[16,1,128,32]{3,0,2,1:T(8,128)S(1)} %copy.77), kind=kOutput, calls=%fused_computation.26 | convolution fusion | flops 25165824 | bytes 1048576 | tf_op jit(solution)/shard_map/wfs,wfc->fsc/dot_general | solution.py:93
  118.4 3.9 %add_bitcast_fusion = f32[1,128,32,32]{3,2,1,0:T(8,128)S(1)} fusion(f32[128,32,32]{2,1,0:T(8,128)S(1)} %fusion.21, f32[16,128,32]{2,0,1:T(8,128)S(1)} %copy-done, f32[16,1,128,32]{3,0,2,1:T(8,128)S(1)} %copy.78), kind=kOutput, calls=%fused_computation.14 | convolution fusion | flops 25296896 | bytes 1572864 | tf_op jit(solution)/shard_map/wfs,wfc->fsc/dot_general | solution.py:92
  122.3 3.7 %subtract_bitcast_fusion = f32[1,128,32,32]{3,2,1,0:T(8,128)S(1)} fusion(f32[128,32,32]{2,1,0:T(8,128)S(1)} %fusion.19, f32[16,128,32]{2,0,1:T(8,128)S(1)} %copy.67, f32[16,1,128,32]{3,0,2,1:T(8,128)S(1)} %copy.78), kind=kOutput, calls=%fused_computation.13 | convolution fusion | flops 25296896 | bytes 1572864 | tf_op jit(solution)/shard_map/wfs,wfc->fsc/dot_general | solution.py:95
  126.0 0.6 pad_maximum_fusion
  126.9 9.1 %fusion.11 = f32[32,256,32]{1,2,0:T(8,128)} fusion(f32[2,128,32,32]{3,2,1,0:T(8,128)S(1)} %pad_maximum_fusion, f32[256,1,128]{2,0,1:T(8,128)S(1)} %copy-done.1, f32[256,1,128]{2,0,1:T(8,128)S(1)} %get-tuple-element.11), kind=kOutput, calls=%fused_computation.19 | convolution fusion | flops 805371904 | bytes 2359296 | tf_op jit(solution)/shard_map/tak,aksc->stc/dot_general | solution.py:103
  136.0 25.6 %reduce-scatter.2.cloned.1.call-done = f32[8,256,32]{1,2,0:T(8,128)} async-done(((f32[32,256,32]{1,2,0:T(8,128)}), f32[8,256,32]{1,2,0:T(8,128)}) %reduce-scatter.2.cloned.1.call-update) | async-done | bytes 262160 | tf_op jit(solution)/shard_map/reduce_scatter | solution.py:102
  (25 shorter events, 1.5 us)
Async XLA Ops:
  8.6 14.9 %all-to-all-start = ((f32[4,128,256]{1,0,2:T(4,128)}), f32[4,128,256]{1,0,2:T(4,128)S(1)}, u32[]{:S(2)}, u32[]{:S(2)}) async-start(f32[4,128,256]{1,0,2:T(4,128)} %copy.58), calls=%async_computation | async-start | bytes 1048576 | tf_op jit(solution)/shard_map/all_to_all | solution.py:58
  69.9 6.9 %copy-start.2 = (s32[32]{0:T(128)S(1)}, s32[32]{0:T(128)}, u32[]{:S(2)}) copy-start(s32[32]{0:T(128)} %param.3) | copy-start | bytes 388
  72.0 19.5 %all-to-all-start.1 = ((f32[4,1,32768]{2,1,0:T(1,128)}), f32[4,1,32768]{2,1,0:T(1,128)S(1)}, u32[]{:S(2)}, u32[]{:S(2)}) async-start(f32[4,1,32768]{2,1,0:T(1,128)} %reshape.201), calls=%async_computation.1 | async-start | bytes 1048576 | tf_op jit(solution)/shard_map/all_to_all | solution.py:72
  76.9 84.7 %reduce-scatter.2.cloned.1.call-start = ((), (), s32[]{:S(2)}) async-start(), calls=%async_computation.3 | async-start | bytes 1310720 | tf_op jit(solution)/shard_map/reduce_scatter | solution.py:102
  111.1 3.6 %copy-start = (f32[16,128,32]{2,0,1:T(8,128)S(1)}, f32[16,128,32]{2,0,1:T(8,128)}, u32[]{:S(2)}) copy-start(f32[16,128,32]{2,0,1:T(8,128)} %copy.69) | copy-start | bytes 786436
  126.0 0.9 copy-start.1
Sparse Core Ops, SparseCore 0:
  136.1 25.3 reduce-scatter.1
where the time goes:
time: 169 us; the launch traced here: 168 us
  other arithmetic  50.1 us (30%)
  waiting for transfers between devices  39.4 us (23%)
  matrix products  31.5 us (19%)
  local copies, waits for them, and re-layouts  13.8 us (8%)
  between operations  13.6 us (8%)
  starting transfers between devices  10.1 us (6%)
  blocking collectives  9.97 us (6%)
    another operation x3, other arithmetic  36.6 us
    reduce_scatter x1, waiting for transfers between devices, local(): lax.psum_scatter(jnp.einsum('tak,aksc->stc', band_table_part, stacked, pr...  25.6 us
    all_to_all x1, waiting for transfers between devices, local(): lax.all_to_all(whitened, 'win', split_axis=2, concat_axis=0, tiled=True)  13.3 us
    all_gather x1, blocking collectives, local(): spectra = lax.all_gather(chosen, 'chan', axis=3, tiled=True)  9.97 us
    neg x1, other arithmetic, fourier_table(): return jnp.concatenate([jnp.cos(angles), -jnp.sin(angles)], axis=0)  9.19 us
    dot_general x1, matrix products, local(): jnp.einsum('tak,aksc->stc', band_table_part, stacked, precision=HIGHEST)  9.09 us
    unnamed x11, local copies, waits for them, and re-layouts  7.61 us
    dot_general x1, matrix products, local(): jnp.einsum('kt,wtc->wkc', forward, whiten_pieces, precision=HIGHEST)  6.57 us
  transfers between devices with their start and end apart: 3, of which 3 were waited for; matrix products, arithmetic and copies ran while one was open for 6% of the time, Pallas kernels for 0%

commit v1 on v0

--- a/solution.py
+++ b/solution.py
@@ -69,7 +69,10 @@
         + WHITE_EPSILON
     )
     whitened = jnp.stack([real_part / smoothed, imag_part / smoothed], axis=1)
-    band_data = lax.all_to_all(whitened, "win", split_axis=2, concat_axis=0, tiled=True)
+    devices = lax.axis_size("win")
+    tiles = jnp.stack(jnp.split(whitened, devices, axis=2), axis=0)
+    tiles = lax.all_to_all(tiles, "win", split_axis=0, concat_axis=0)
+    band_data = jnp.concatenate(tiles, axis=0)
     total_windows = band_data.shape[0]
     band_count = band_data.shape[2]
     source_count = sources.shape[0]

time: 169 us -> 162 us (0.959)
  local copies, waits for them, and re-layouts: 13.8 us -> 8.23 us
    all_to_all x1 -> x0, other arithmetic: 2.14 us -> none  [local(): lax.all_to_all(whitened, 'win', split_axis=2, concat_axis=0, tiled=True)]
    squeeze x3 -> x0, local copies, waits for them, and re-layouts: 1.9 us -> none  [the longest x1 1.36 us: local(): white_imag = band_data[:, 1]]
    another operation x4 -> x5, other arithmetic: 36.7 us -> 37.5 us
  transfers between devices with their start and end apart: 3 -> 3, of which waited for: 3 -> 3; matrix products, arithmetic and copies ran while one was open for 6% -> 7% of each run, Pallas kernels for 0% -> 0%
where the time goes in v1:
time: 162 us
  other arithmetic  48.8 us (30%)
  waiting for transfers between devices  39.4 us (24%)
  matrix products  31.5 us (19%)
  between operations  13.6 us (8%)
  blocking collectives  10.2 us (6%)
  starting transfers between devices  10.1 us (6%)
  local copies, waits for them, and re-layouts  8.23 us (5%)
    another operation x3, other arithmetic  36.6 us
    reduce_scatter x1, waiting for transfers between devices, local(): lax.psum_scatter(jnp.einsum('tak,aksc->stc', band_table_part, stacked, pr...  25.6 us
    all_to_all x1, waiting for transfers between devices, local(): tiles = lax.all_to_all(tiles, 'win', split_axis=0, concat_axis=0)  13.2 us
    all_gather x1, blocking collectives, local(): spectra = lax.all_gather(chosen, 'chan', axis=3, tiled=True)  10.2 us
    neg x1, other arithmetic, fourier_table(): return jnp.concatenate([jnp.cos(angles), -jnp.sin(angles)], axis=0)  9.17 us
    dot_general x1, matrix products, local(): jnp.einsum('tak,aksc->stc', band_table_part, stacked, precision=HIGHEST)  9.09 us
    dot_general x1, matrix products, local(): jnp.einsum('kt,wtc->wkc', forward, whiten_pieces, precision=HIGHEST)  6.57 us
    unnamed x11, local copies, waits for them, and re-layouts  6.26 us
  transfers between devices with their start and end apart: 3, of which 3 were waited for; matrix products, arithmetic and copies ran while one was open for 7% of the time, Pallas kernels for 0%

profile of v1, /device:TPU:0, one launch (start us, length us, event | category | flops | bytes accessed | tf_op | source)
XLA Modules:
  0.0 161.8 jit_solution(16420873942070988072)
XLA Ops:
  6.5 2.1 %copy.50 = f32[4,128,256]{1,0,2:T(4,128)} copy(f32[4,128,256]{2,1,0:T(8,128)} %param.2) | data formatting | bytes 1048576 | tf_op args[0]
  8.6 5.2 %all-to-all-start = ((f32[4,128,256]{1,0,2:T(4,128)}), f32[4,128,256]{1,0,2:T(4,128)S(1)}, u32[]{:S(2)}, u32[]{:S(2)}) async-start(f32[4,128,256]{1,0,2:T(4,128)} %copy.50), calls=%async_computation | async-start | bytes 1048576 | tf_op jit(solution)/shard_map/all_to_all | solution.py:58
  13.8 9.2 %sine_negate_fusion = (f32[512,1024]{1,0:T(8,128)}, f32[512,1024]{1,0:T(8,128)}) fusion(), kind=kLoop, calls=%fused_computation.15 | loop fusion | flops 7864320 | bytes 4194304 | tf_op jit(solution)/shard_map/neg | solution.py:17
  23.0 0.5 all-to-all-done
  23.6 0.2 abs_bitcast_fusion
  24.0 36.3 %reduce-window.6 = f32[4,32,9,128]{3,2,1,0:T(8,128)S(1)} reduce-window(f32[4,32,9,128]{3,2,1,0:T(8,128)S(1)} %reshape.197, f32[]{:T(128)} %constant.22.clone.1), window={size=1x1x1x128 pad=0_0x0_0x0_0x127_0}, to_apply=%region_0.1 | reduce-window | flops 18726912 | bytes 1179652 | tf_op jit(solution)/shard_map/reduce-window
  60.2 0.3 slice.45
  60.6 0.4 copy.53
  61.0 0.1 copy.54
  61.1 0.3 broadcast_add_fusion
  61.4 0.1 reduce_window_sum.16
  61.5 6.6 %fusion.14 = f32[4,1024,32]{1,2,0:T(8,128)S(1)} fusion(f32[512,1024]{1,0:T(8,128)} %get-tuple-element.17, f32[512,1024]{1,0:T(8,128)} %get-tuple-element.18, f32[4,1056,32]{1,2,0:T(8,128)S(1)} %bitcast.90, f32[4,1152,32]{1,2,0:T(8,128)S(1)} %bitcast.89, f32[4,8,4,8,128]{4,3,2,1,0:T(8,128)S(1)} %bitcast.87), kind=kOutput, calls=%fused_computation.20 | convolution fusion | flops 1612185600 | bytes 6356992 | tf_op jit(solution)/shard_map/kt,wtc->wkc/dot_general | solution.py:62
  68.1 0.7 divide_bitcast_fusion.1
  68.9 0.9 pad_maximum_fusion.1
  69.7 4.9 %all-to-all-start.1 = ((f32[4,4,2,128,32]{3,4,1,2,0:T(8,128)}), f32[4,4,2,128,32]{3,4,1,2,0:T(8,128)S(1)}, u32[]{:S(2)}, u32[]{:S(2)}) async-start(f32[4,4,2,128,32]{3,4,1,2,0:T(8,128)} %pad_maximum_fusion.1), calls=%async_computation.1 | async-start | bytes 1048576 | tf_op jit(solution)/shard_map/all_to_all | solution.py:74
  74.7 1.3 cosine_multiply_fusion
  76.0 13.2 %all-to-all-done.1 = f32[4,4,2,128,32]{3,4,1,2,0:T(8,128)S(1)} async-done(((f32[4,4,2,128,32]{3,4,1,2,0:T(8,128)}), f32[4,4,2,128,32]{3,4,1,2,0:T(8,128)S(1)}, u32[]{:S(2)}, u32[]{:S(2)}) %all-to-all-start.1) | async-done | bytes 524320 | tf_op jit(solution)/shard_map/all_to_all | solution.py:74
  89.3 0.3 fusion.60
  89.6 10.2 %all_gather.3 = f32[16,2,128,32]{2,0,1,3:T(8,128)S(1)} all-gather(f32[16,2,128,4]{2,0,1,3:T(8,128)S(1)} %copy.56), channel_id=1, replica_groups=mesh['chan'=8,'win'=4] {'chan'}, dimensions={3}, use_global_device_ids=true | all-gather | bytes 589824 | tf_op jit(solution)/shard_map/all_gather | solution.py:88
  99.8 0.7 fusion.72
  100.5 0.5 copy.66
  101.1 0.5 copy.67
  101.6 1.5 copy.68
  103.1 1.4 copy.69
  104.4 3.6 %fusion.23 = f32[128,32,32]{2,1,0:T(8,128)S(1)} fusion(f32[16,1,128,32]{3,0,2,1:T(8,128)S(1)} %copy.67, f32[16,1,128,32]{3,0,2,1:T(8,128)S(1)} %copy.66), kind=kOutput, calls=%fused_computation.30 | convolution fusion | flops 25165824 | bytes 1048576 | tf_op jit(solution)/shard_map/wfs,wfc->fsc/dot_general | solution.py:93
  108.1 3.6 %fusion.17 = f32[128,32,32]{2,1,0:T(8,128)S(1)} fusion(f32[16,1,128,32]{3,0,2,1:T(8,128)S(1)} %copy-done, f32[16,1,128,32]{3,0,2,1:T(8,128)S(1)} %copy.66), kind=kOutput, calls=%fused_computation.24 | convolution fusion | flops 25165824 | bytes 1048576 | tf_op jit(solution)/shard_map/wfs,wfc->fsc/dot_general | solution.py:96
  111.7 3.9 %add_bitcast_fusion = f32[1,128,32,32]{3,2,1,0:T(8,128)S(1)} fusion(f32[128,32,32]{2,1,0:T(8,128)S(1)} %fusion.23, f32[16,1,128,32]{3,0,2,1:T(8,128)S(1)} %copy-done, f32[16,1,128,32]{3,0,2,1:T(8,128)S(1)} %copy.68), kind=kOutput, calls=%fused_computation.14 | convolution fusion | flops 25296896 | bytes 1572864 | tf_op jit(solution)/shard_map/wfs,wfc->fsc/dot_general | solution.py:95
  115.6 3.7 %subtract_bitcast_fusion = f32[1,128,32,32]{3,2,1,0:T(8,128)S(1)} fusion(f32[128,32,32]{2,1,0:T(8,128)S(1)} %fusion.17, f32[16,1,128,32]{3,0,2,1:T(8,128)S(1)} %copy.68, f32[16,1,128,32]{3,0,2,1:T(8,128)S(1)} %copy.67), kind=kOutput, calls=%fused_computation.13 | convolution fusion | flops 25296896 | bytes 1572864 | tf_op jit(solution)/shard_map/wfs,wfc->fsc/dot_general | solution.py:98
  119.3 0.6 pad_maximum_fusion
  119.9 0.3 copy-done.1
  120.2 9.1 %fusion.11 = f32[32,256,32]{1,2,0:T(8,128)} fusion(f32[2,128,32,32]{3,2,1,0:T(8,128)S(1)} %pad_maximum_fusion, f32[256,1,128]{2,0,1:T(8,128)S(1)} %copy-done.1, f32[256,1,128]{2,0,1:T(8,128)S(1)} %get-tuple-element.15), kind=kOutput, calls=%fused_computation.19 | convolution fusion | flops 805371904 | bytes 2359296 | tf_op jit(solution)/shard_map/tak,aksc->stc/dot_general | solution.py:106
  129.4 25.6 %reduce-scatter.2.cloned.1.call-done = f32[8,256,32]{1,2,0:T(8,128)} async-done(((f32[32,256,32]{1,2,0:T(8,128)}), f32[8,256,32]{1,2,0:T(8,128)}) %reduce-scatter.2.cloned.1.call-update) | async-done | bytes 262160 | tf_op jit(solution)/shard_map/reduce_scatter | solution.py:105
  (21 shorter events, 0.5 us)
Async XLA Ops:
  8.6 14.9 %all-to-all-start = ((f32[4,128,256]{1,0,2:T(4,128)}), f32[4,128,256]{1,0,2:T(4,128)S(1)}, u32[]{:S(2)}, u32[]{:S(2)}) async-start(f32[4,128,256]{1,0,2:T(4,128)} %copy.50), calls=%async_computation | async-start | bytes 1048576 | tf_op jit(solution)/shard_map/all_to_all | solution.py:58
  68.8 5.8 %copy-start.2 = (s32[32]{0:T(128)S(1)}, s32[32]{0:T(128)}, u32[]{:S(2)}) copy-start(s32[32]{0:T(128)} %param.3) | copy-start | bytes 388
  69.7 19.5 %all-to-all-start.1 = ((f32[4,4,2,128,32]{3,4,1,2,0:T(8,128)}), f32[4,4,2,128,32]{3,4,1,2,0:T(8,128)S(1)}, u32[]{:S(2)}, u32[]{:S(2)}) async-start(f32[4,4,2,128,32]{3,4,1,2,0:T(8,128)} %pad_maximum_fusion.1), calls=%async_computation.1 | async-start | bytes 1048576 | tf_op jit(solution)/shard_map/all_to_all | solution.py:74
  74.6 80.3 %reduce-scatter.2.cloned.1.call-start = ((), (), s32[]{:S(2)}) async-start(), calls=%async_computation.3 | async-start | bytes 1310720 | tf_op jit(solution)/shard_map/reduce_scatter | solution.py:105
  104.4 3.6 %copy-start = (f32[16,1,128,32]{3,0,2,1:T(8,128)S(1)}, f32[16,1,128,32]{3,0,2,1:T(8,128)}, u32[]{:S(2)}) copy-start(f32[16,1,128,32]{3,0,2,1:T(8,128)} %copy.69) | copy-start | bytes 786436
  119.3 0.9 copy-start.1
Sparse Core Ops, SparseCore 0:
  129.5 25.4 reduce-scatter.1
